TPU v7x, 32 devices: a whole 2x2x4 slice. The times are simulated.
32 devices in a mesh: grp: 2 (over y), ia: 4 (over x, core), ja: 4 (over z).
Axes of the slice: x: 2, y: 2, z: 4, core: 2. Of those that a mesh axis runs over, the one named last changes fastest.
Arguments:
- amplitudes: float32 [16, 8, 160, 160], P(('grp', 'ia'), 'ja'), parts along dimension 0, may hold values from -3 to 3
- integrals: float32 [16, 8, 160, 160], P(('grp', 'ia'), 'ja'), parts along dimension 0, may hold values from -6 to 6
- row_intersection: float32 [16, 8, 8, 160, 160], P(('grp', 'ia'), 'ja'), parts along dimension 0, as said below
- column_intersection: float32 [16, 8, 8, 160, 160], P(('grp', 'ia'), 'ja'), parts along dimension 0, as said below
- row_tiles: int32 [16, 8], P(('grp', 'ia')), parts along dimension 0, may hold values from 0 to 7, as said below
- row_coupling: float32 [16, 8], P(('grp', 'ia')), parts along dimension 0, may hold values from 0.02 to 0.12
- row_counts: int32 [16], P(('grp', 'ia')), parts along dimension 0, may hold values from 1 to 8, as said below
- column_tiles: int32 [16, 8], P(('grp', 'ja')), parts along dimension 0, may hold values from 0 to 7, as said below
- column_coupling: float32 [16, 8], P(('grp', 'ja')), parts along dimension 0, may hold values from 0.02 to 0.12
- column_counts: int32 [16], P(('grp', 'ja')), parts along dimension 0, may hold values from 1 to 8, as said below
- virtual_energy: float32 [16, 8, 160], P(('grp', 'ia'), 'ja'), parts along dimension 0, may hold values from 0.5 to 3
- first_energy: float32 [16], P(('grp', 'ia')), parts along dimension 0, may hold values from -1.5 to -0.3
- second_energy: float32 [16], P(('grp', 'ja')), parts along dimension 0, may hold values from -1.5 to -0.3
Outputs:
- new_amplitudes: float32 [16, 8, 160, 160], P(('grp', 'ia'), 'ja'), parts along dimension 0
- last_residual: float32 [16, 8, 160, 160], P(('grp', 'ia'), 'ja'), parts along dimension 0
There are 2 independent parts, one for each index of `grp`. A program takes and returns all parts, laid end to end along the dimension named above; each array names one. Nothing has to cross between parts.
Inputs may be any that keep to these rules, and one draw needn't show every extreme that they name: `row_tiles`: each row holds 8 different first-fragment orbitals. `column_tiles`: each row holds 8 different second-fragment orbitals. `row_counts`: some orbital has all 8 slots live. `column_counts`: some orbital has all 8 slots live. `row_intersection`: identity plus an independent perturbation of full rank. `column_intersection`: identity plus an independent perturbation of full rank.
All inputs are finite; a program needn't handle non-finite values.
Results may differ from a plain program's by a relative error of at most 0.00017.
Values sent between devices are 32-bit elements; how exact they have to be, the bound alone decides.
No kernel may reach another device: no remote copies, remote signals or barrier semaphores. Data moves between devices by JAX's collectives and lax.ppermute only.
A program may use at most 128 MiB of HBM per device.

v0:
```python
import jax
import jax.numpy as jnp
from jax import lax
from jax.sharding import PartitionSpec as P

ITERS = 2


def sandwich(intersection, block):
    left = jnp.matmul(intersection, block, precision=lax.Precision.HIGHEST)
    return jnp.matmul(left, jnp.swapaxes(intersection, -1, -2), precision=lax.Precision.HIGHEST)


def coupled_sum(intersection, chosen, weight, counts, row_side):
    longest = jnp.max(counts)

    def one_slot(slot, total):
        over_slot = lax.dynamic_index_in_dim(intersection, slot, 2, keepdims=False)
        chosen_slot = lax.dynamic_index_in_dim(chosen, slot, 2, keepdims=False)
        weight_slot = lax.dynamic_index_in_dim(weight, slot, 1, keepdims=False)
        product = sandwich(over_slot, chosen_slot)
        if row_side:
            scaled = weight_slot[:, None, None, None] * product
        else:
            scaled = weight_slot[None, :, None, None] * product
        return total + scaled

    start = jnp.zeros(chosen.shape[:2] + chosen.shape[3:], jnp.float32)
    return lax.fori_loop(0, longest, one_slot, start)


def local(
    amplitudes,
    integrals,
    row_intersection,
    column_intersection,
    row_tiles,
    row_coupling,
    row_counts,
    column_tiles,
    column_coupling,
    column_counts,
    virtual_energy,
    first_energy,
    second_energy,
):
    denom = (
        virtual_energy[:, :, :, None]
        + virtual_energy[:, :, None, :]
        - first_energy[:, None, None, None]
        - second_energy[None, :, None, None]
    )
    slot_index = jnp.arange(row_tiles.shape[1], dtype=jnp.int32)
    row_weight = row_coupling * (slot_index[None, :] < row_counts[:, None]).astype(jnp.float32)
    column_weight = column_coupling * (slot_index[None, :] < column_counts[:, None]).astype(
        jnp.float32
    )
    current = amplitudes
    residual = jnp.zeros_like(amplitudes)
    for iteration in range(ITERS):
        gathered_rows = lax.all_gather(current, "ia", axis=0, tiled=True)
        gathered_columns = lax.all_gather(current, "ja", axis=1, tiled=True)
        row_chosen = jnp.swapaxes(gathered_rows[row_tiles], 1, 2)
        column_chosen = gathered_columns[:, column_tiles]
        row_term = coupled_sum(row_intersection, row_chosen, row_weight, row_counts, True)
        column_term = coupled_sum(
            column_intersection, column_chosen, column_weight, column_counts, False
        )
        residual = integrals + denom * current - row_term - column_term
        current = current - residual / denom
    return (current, residual)


def solution(mesh):
    placed = (
        P(("grp", "ia"), "ja", None, None),
        P(("grp", "ia"), "ja", None, None),
        P(("grp", "ia"), "ja", None, None, None),
        P(("grp", "ia"), "ja", None, None, None),
        P(("grp", "ia"), None),
        P(("grp", "ia"), None),
        P(("grp", "ia")),
        P(("grp", "ja"), None),
        P(("grp", "ja"), None),
        P(("grp", "ja")),
        P(("grp", "ia"), "ja", None),
        P(("grp", "ia")),
        P(("grp", "ja")),
    )
    return jax.shard_map(
        local,
        mesh=mesh,
        in_specs=placed,
        out_specs=(P(("grp", "ia"), "ja", None, None), P(("grp", "ia"), "ja", None, None)),
        check_vma=False,
    )
```

profile of v0, /device:TPU:16, one launch (start us, length us, event | category | flops | bytes accessed | tf_op | source)
XLA Modules:
  0.0 275.3 jit_solution(13624956626482143141)
XLA Ops:
  9.5 5.4 %copy.44 = f32[2,2,8,160,160]{4,3,1,0,2:T(8,128)} copy(f32[2,2,8,160,160]{4,3,2,1,0:T(8,128)} %param.23) | data formatting | bytes 6553600 | tf_op jit(solution)/shard_map/while | solution.py:29
  15.1 5.6 %copy.47 = f32[2,2,8,160,160]{4,3,1,0,2:T(8,128)} copy(f32[2,2,8,160,160]{4,3,2,1,0:T(8,128)} %param.24) | data formatting | bytes 6553600 | tf_op jit(solution)/shard_map/while | solution.py:29
  22.1 14.0 %all-gather.5.cloned.1.call-done = f32[8,2,160,160]{3,2,1,0:T(8,128)} async-done(((f32[2,2,160,160]{3,2,1,0:T(8,128)}), f32[8,2,160,160]{3,2,1,0:T(8,128)}) %all-gather.5.cloned.1.call-update) | async-done | bytes 1638416 | tf_op jit(solution)/shard_map/all_gather | solution.py:61
  36.2 5.0 %gather_fusion = f32[16,2,160,160]{3,2,1,0:T(8,128)} fusion(f32[8,2,160,160]{3,2,1,0:T(8,128)} %all-gather.5.cloned.1.call-done, s32[1024]{0:T(1024)S(1)} %pad_clamp_fusion.1), kind=kCustom, calls=%fused_computation | custom fusion | bytes 6553664 | tf_op jit(solution)/shard_map/gather | solution.py:63
  41.2 34.7 %while.40 = (s32[]{:T(128)}, f32[2,2,160,160]{3,2,1,0:T(8,128)S(1)}, s32[]{:T(128)}, f32[2,8]{0,1:T(8,128)S(1)}, f32[2,2,8,160,160]{4,3,1,0,2:T(8,128)}, /*index...) while((s32[]{:T(128)}, f32[2,2,160,160]{3,2,1,0:T(8,128)S(1)}, s32[]{:T(128)}, ...), condition=%wide.region_2.3_spmd, body=%wide.region_1.2_spmd.sunk | while | flops 393420800 | bytes 3605663 | solution.py:29
  44.0 2.1 fusion.81
  46.8 2.1 fusion.79
  48.9 2.1 fusion.81
  53.8 2.1 fusion.81
  56.5 2.1 fusion.79
  58.6 2.1 fusion.81
  63.5 2.1 fusion.81
  68.3 2.1 fusion.81
  71.1 2.1 fusion.79
  73.2 2.1 fusion.81
  75.9 15.4 %all-gather.7.cloned.1.call-done = f32[2,8,160,160]{3,2,1,0:T(8,128)} async-done(((f32[2,2,160,160]{3,2,1,0:T(8,128)}), f32[2,8,160,160]{3,2,1,0:T(8,128)}) %all-gather.7.cloned.1.call-update) | async-done | bytes 1638416 | tf_op jit(solution)/shard_map/all_gather | solution.py:62
  91.3 5.0 %gather_fusion.1 = f32[16,2,160,160]{3,2,1,0:T(8,128)} fusion(f32[2,8,160,160]{3,2,1,0:T(8,128)} %all-gather.7.cloned.1.call-done, s32[1024]{0:T(1024)S(1)} %pad_clamp_fusion), kind=kCustom, calls=%fused_computation.1 | custom fusion | bytes 6553664 | tf_op jit(solution)/shard_map/gather | solution.py:64
  96.4 39.2 %while.41 = (s32[]{:T(128)}, f32[2,2,160,160]{3,2,1,0:T(8,128)S(1)}, s32[]{:T(128)}, f32[2,8]{0,1:T(8,128)S(1)}, f32[2,2,8,160,160]{4,3,1,0,2:T(8,128)}, /*index...) while((s32[]{:T(128)}, f32[2,2,160,160]{3,2,1,0:T(8,128)S(1)}, s32[]{:T(128)}, ...), condition=%wide.region_5.6_spmd, body=%wide.region_4.5_spmd.sunk | while | flops 393420800 | bytes 3605663 | solution.py:29
  99.2 2.1 fusion.87
  104.0 2.1 fusion.87
  108.8 2.1 fusion.87
  113.6 2.1 fusion.87
  118.4 2.1 fusion.87
  123.2 2.1 fusion.87
  128.0 2.1 fusion.87
  132.8 2.1 fusion.87
  137.3 25.0 %all-gather.9.cloned.1.call-done = f32[8,2,160,160]{3,2,1,0:T(8,128)} async-done(((f32[2,2,160,160]{3,2,1,0:T(8,128)}), f32[8,2,160,160]{3,2,1,0:T(8,128)}) %all-gather.9.cloned.1.call-update) | async-done | bytes 1638416 | tf_op jit(solution)/shard_map/all_gather | solution.py:61
  162.3 4.9 %gather_fusion.2 = f32[16,2,160,160]{3,2,1,0:T(8,128)} fusion(f32[8,2,160,160]{3,2,1,0:T(8,128)} %all-gather.9.cloned.1.call-done, s32[1024]{0:T(1024)S(1)} %pad_clamp_fusion.1), kind=kCustom, calls=%fused_computation.2 | custom fusion | bytes 6553664 | tf_op jit(solution)/shard_map/gather | solution.py:63
  167.2 5.4 %copy.60 = f32[2,8,2,160,160]{4,3,2,0,1:T(8,128)} copy(f32[2,8,2,160,160]{4,3,2,1,0:T(8,128)} %bitcast.100) | data formatting | bytes 6553600 | tf_op jit(solution)/shard_map/gather | solution.py:63
  172.6 34.7 %while.42 = (s32[]{:T(128)}, f32[2,2,160,160]{3,2,1,0:T(8,128)S(1)}, s32[]{:T(128)}, f32[2,8]{0,1:T(8,128)S(1)}, f32[2,2,8,160,160]{4,3,1,0,2:T(8,128)}, /*index...) while((s32[]{:T(128)}, f32[2,2,160,160]{3,2,1,0:T(8,128)S(1)}, s32[]{:T(128)}, ...), condition=%wide.region_7.8_spmd, body=%wide.region_6.7_spmd.sunk | while | flops 393420800 | bytes 3605663 | solution.py:29
  173.3 2.1 fusion.92
  175.5 2.1 fusion.94
  180.3 2.1 fusion.94
  183.1 2.1 fusion.92
  185.2 2.1 fusion.94
  190.0 2.1 fusion.94
  194.9 2.1 fusion.94
  197.6 2.1 fusion.92
  199.7 2.1 fusion.94
  204.6 2.1 fusion.94
  207.3 10.6 %all-gather.11.cloned.1.call-done = f32[2,8,160,160]{3,2,1,0:T(8,128)} async-done(((f32[2,2,160,160]{3,2,1,0:T(8,128)}), f32[2,8,160,160]{3,2,1,0:T(8,128)}) %all-gather.11.cloned.1.call-update) | async-done | bytes 1638416 | tf_op jit(solution)/shard_map/all_gather | solution.py:62
  217.9 5.0 %gather_fusion.3 = f32[16,2,160,160]{3,2,1,0:T(8,128)} fusion(f32[2,8,160,160]{3,2,1,0:T(8,128)} %all-gather.11.cloned.1.call-done, s32[1024]{0:T(1024)S(1)} %pad_clamp_fusion), kind=kCustom, calls=%fused_computation.3 | custom fusion | bytes 6553664 | tf_op jit(solution)/shard_map/gather | solution.py:64
  222.8 5.4 %copy.59 = f32[2,8,2,160,160]{4,3,0,2,1:T(8,128)} copy(f32[2,8,2,160,160]{4,3,2,1,0:T(8,128)} %bitcast.101) | data formatting | bytes 6553600 | tf_op jit(solution)/shard_map/gather | solution.py:64
  228.3 39.1 %while.43 = (s32[]{:T(128)}, f32[2,2,160,160]{3,2,1,0:T(8,128)S(1)}, s32[]{:T(128)}, f32[2,8]{0,1:T(8,128)S(1)}, f32[2,2,8,160,160]{4,3,1,0,2:T(8,128)}, /*index...) while((s32[]{:T(128)}, f32[2,2,160,160]{3,2,1,0:T(8,128)S(1)}, s32[]{:T(128)}, ...), condition=%wide.region_9.10_spmd, body=%wide.region_8.9_spmd.sunk | while | flops 393420800 | bytes 3605663 | solution.py:29
  231.1 2.1 fusion.101
  235.9 2.1 fusion.101
  245.5 2.1 fusion.101
  259.9 2.1 fusion.101
  (106 shorter events, 64.9 us)
Async XLA Ops:
  7.2 29.0 %all-gather.5.cloned.1.call-start = ((), (), s32[]{:S(2)}) async-start(), calls=%async_computation | async-start | bytes 3276800 | tf_op jit(solution)/shard_map/all_gather | solution.py:61
  7.9 83.4 %all-gather.7.cloned.1.call-start = ((), (), s32[]{:S(2)}) async-start(), calls=%async_computation.1 | async-start | bytes 3276800 | tf_op jit(solution)/shard_map/all_gather | solution.py:62
  8.6 153.7 %all-gather.9.cloned.1.call-start = ((), (), s32[]{:S(2)}) async-start(), calls=%async_computation.2 | async-start | bytes 3276800 | tf_op jit(solution)/shard_map/all_gather | solution.py:61
  9.5 5.4 %copy-start.6 = (f32[2,8]{1,0:T(2,128)S(1)}, f32[2,8]{1,0:T(2,128)}, u32[]{:S(2)}) copy-start(f32[2,8]{1,0:T(2,128)} %param.26) | copy-start | bytes 196
  9.5 5.5 %copy-start.8 = (s32[2,8]{1,0:T(2,128)S(1)}, s32[2,8]{1,0:T(2,128)}, u32[]{:S(2)}) copy-start(s32[2,8]{1,0:T(2,128)} %param.28) | copy-start | bytes 196
  15.1 5.6 %copy-start.7 = (f32[2,8]{1,0:T(2,128)S(1)}, f32[2,8]{1,0:T(2,128)}, u32[]{:S(2)}) copy-start(f32[2,8]{1,0:T(2,128)} %param.29) | copy-start | bytes 196
  15.1 5.7 %copy-start.9 = (s32[2]{0:T(128)S(1)}, s32[2]{0:T(128)}, u32[]{:S(2)}) copy-start(s32[2]{0:T(128)} %param.27) | copy-start | bytes 28
  15.1 6.4 %copy-start.10 = (s32[2]{0:T(128)S(1)}, s32[2]{0:T(128)}, u32[]{:S(2)}) copy-start(s32[2]{0:T(128)} %param.30) | copy-start | bytes 28
  96.3 39.2 %copy-start.1 = (f32[2,2,160,160]{3,2,1,0:T(8,128)S(1)}, f32[2,2,160,160]{3,2,1,0:T(8,128)}, u32[]{:S(2)}) copy-start(f32[2,2,160,160]{3,2,1,0:T(8,128)} %param.21) | copy-start | bytes 1228804
  96.3 39.2 %copy-start.2 = (f32[2,2,160,160]{3,2,1,0:T(8,128)S(1)}, f32[2,2,160,160]{3,2,1,0:T(8,128)}, u32[]{:S(2)}) copy-start(f32[2,2,160,160]{3,2,1,0:T(8,128)} %param.22) | copy-start | bytes 1228804
  96.3 39.2 %copy-start.3 = (f32[2,2,160]{2,1,0:T(2,128)S(1)}, f32[2,2,160]{2,1,0:T(2,128)}, u32[]{:S(2)}) copy-start(f32[2,2,160]{2,1,0:T(2,128)} %param.31) | copy-start | bytes 7684
  96.4 39.2 %copy-start.4 = (f32[2]{0:T(128)S(1)}, f32[2]{0:T(128)}, u32[]{:S(2)}) copy-start(f32[2]{0:T(128)} %param.33) | copy-start | bytes 28
  96.4 39.2 %copy-start.5 = (f32[2]{0:T(128)S(1)}, f32[2]{0:T(128)}, u32[]{:S(2)}) copy-start(f32[2]{0:T(128)} %param.32) | copy-start | bytes 28
  136.8 81.1 %all-gather.11.cloned.1.call-start = ((), (), s32[]{:S(2)}) async-start(), calls=%async_computation.3 | async-start | bytes 3276800 | tf_op jit(solution)/shard_map/all_gather | solution.py:62
  228.3 39.2 %copy-start = (f32[2,2,160,160]{3,2,1,0:T(8,128)S(1)}, f32[2,2,160,160]{3,2,1,0:T(8,128)}, u32[]{:S(2)}) copy-start(f32[2,2,160,160]{3,2,1,0:T(8,128)} %divide_subtract_fusion.1) | copy-start | bytes 1228804
Sparse Core Ops, SparseCore 0:
  9.5 26.5 all-gather.4
  37.7 53.5 all-gather.6
  136.9 25.3 all-gather.8
  164.3 53.5 all-gather.10
where the time goes:
time: 278 us; the launch traced here: 275 us
  matrix products  123 us (44%)
  waiting for transfers between devices  66.9 us (24%)
  local copies, waits for them, and re-layouts  42.4 us (15%)
  loops' own time  24 us (9%)
  between operations  14 us (5%)
  other arithmetic  4.52 us (2%)
    dot_general x30, matrix products, sandwich(): left = jnp.matmul(intersection, block, precision=lax.Precision.HIGHEST)  61.7 us
    dot_general x30, matrix products, sandwich(): jnp.matmul(left, jnp.swapaxes(intersection, -1, -2), precision=lax.Precis...  61.7 us
    all_gather x2, waiting for transfers between devices, local(): gathered_rows = lax.all_gather(current, 'ia', axis=0, tiled=True)  39 us
    all_gather x2, waiting for transfers between devices, local(): gathered_columns = lax.all_gather(current, 'ja', axis=1, tiled=True)  26 us
    another operation x4, loops' own time, coupled_sum(): return lax.fori_loop(0, longest, one_slot, start)  24 us
    gather x3, local copies, waits for them, and re-layouts, local(): column_chosen = gathered_columns[:, column_tiles]  15.3 us
    gather x3, local copies, waits for them, and re-layouts, local(): row_chosen = jnp.swapaxes(gathered_rows[row_tiles], 1, 2)  15.2 us
    while x2, local copies, waits for them, and re-layouts, coupled_sum(): return lax.fori_loop(0, longest, one_slot, start)  11 us
  transfers between devices with their start and end apart: 4, of which 4 were waited for; matrix products, arithmetic and copies ran while one was open for 31% of the time, Pallas kernels for 0%

commit v1 on v0

--- a/solution.py
+++ b/solution.py
@@ -2,8 +2,45 @@
 import jax.numpy as jnp
 from jax import lax
 from jax.sharding import PartitionSpec as P
+from jax.lax import axis_index, axis_size, ppermute
 
 ITERS = 2
+
+
+def _build_keys(message, group_axis, dimension_no):
+    carry_in, raw_out, z1 = (
+        axis_size(group_axis),
+        axis_index(group_axis),
+        message.shape[dimension_no],
+    )
+    shelf = tuple(
+        (ix * carry_in if k0 == dimension_no else ix for k0, ix in enumerate(message.shape))
+    )
+    response = lax.dynamic_update_slice_in_dim(
+        jnp.zeros(shelf, message.dtype), message, raw_out * z1, axis=dimension_no
+    )
+    frame_out = current_value = message
+    u = 1
+    while u < carry_in // 2 + 1:
+        frame_out = ppermute(
+            frame_out,
+            axis_name=group_axis,
+            perm=tuple(((k0, (k0 + 1) % carry_in) for k0 in range(carry_in))),
+        )
+        response = lax.dynamic_update_slice_in_dim(
+            response, frame_out, (raw_out - u) % carry_in * z1, axis=dimension_no
+        )
+        if 2 * u < carry_in:
+            current_value = ppermute(
+                current_value,
+                axis_name=group_axis,
+                perm=tuple(((k0, (k0 - 1) % carry_in) for k0 in range(carry_in))),
+            )
+            response = lax.dynamic_update_slice_in_dim(
+                response, current_value, (raw_out + u) % carry_in * z1, axis=dimension_no
+            )
+        u = u + 1
+    return response
 
 
 def sandwich(intersection, block):
@@ -59,7 +96,7 @@
     residual = jnp.zeros_like(amplitudes)
     for iteration in range(ITERS):
         gathered_rows = lax.all_gather(current, "ia", axis=0, tiled=True)
-        gathered_columns = lax.all_gather(current, "ja", axis=1, tiled=True)
+        gathered_columns = _build_keys(current, "ja", 1)
         row_chosen = jnp.swapaxes(gathered_rows[row_tiles], 1, 2)
         column_chosen = gathered_columns[:, column_tiles]
         row_term = coupled_sum(row_intersection, row_chosen, row_weight, row_counts, True)

time: 278 us -> 297 us (1.068)
  the two profiles are of different devices: /device:TPU:16 before, /device:TPU:19 now
where the time goes in v1:
time: 297 us; the launch traced here: 294 us
  matrix products  131 us (44%)
  waiting for transfers between devices  56.8 us (19%)
  local copies, waits for them, and re-layouts  55.4 us (19%)
  loops' own time  25.5 us (9%)
  between operations  14.3 us (5%)
  other arithmetic  6.34 us (2%)
  starting transfers between devices  4.47 us (2%)
    dot_general x32, matrix products, sandwich(): jnp.matmul(left, jnp.swapaxes(intersection, -1, -2), precision=lax.Precis...  65.7 us
    dot_general x32, matrix products, sandwich(): left = jnp.matmul(intersection, block, precision=lax.Precision.HIGHEST)  65.6 us
    ppermute x4, waiting for transfers between devices, _build_keys(): ppermute(frame_out, axis_name=group_axis, perm=tuple(((k0, (k0 + 1) % car...  56.7 us
    another operation x4, loops' own time, coupled_sum(): return lax.fori_loop(0, longest, one_slot, start)  25.5 us
    gather x4, local copies, waits for them, and re-layouts, local(): column_chosen = gathered_columns[:, column_tiles]  18.8 us
    gather x3, local copies, waits for them, and re-layouts, local(): row_chosen = jnp.swapaxes(gathered_rows[row_tiles], 1, 2)  15.3 us
    while x2, local copies, waits for them, and re-layouts, coupled_sum(): return lax.fori_loop(0, longest, one_slot, start)  10.8 us
  transfers between devices with their start and end apart: 8, of which 4 were waited for; matrix products, arithmetic and copies ran while one was open for 37% of the time, Pallas kernels for 0%

profile of v1, /device:TPU:19, one launch (start us, length us, event | category | flops | bytes accessed | tf_op | source)
XLA Modules:
  0.0 294.2 jit_solution(18247868047478618065)
XLA Ops:
  13.8 9.5 %collective-permute-done = f32[2,2,160,160]{3,2,1,0:T(8,128)S(1)} collective-permute-done((f32[2,2,160,160]{3,2,1,0:T(8,128)}, f32[2,2,160,160]{3,2,1,0:T(8,128)S(1)}, u32[]{:S(2)}, u32[]{:S(2)}) %collective-permute-start) | collective-permute-done | bytes 409632 | tf_op jit(solution)/shard_map/ppermute | solution.py:25
  27.5 5.4 %copy.37 = f32[2,2,8,160,160]{4,3,1,0,2:T(8,128)} copy(f32[2,2,8,160,160]{4,3,2,1,0:T(8,128)} %param.24) | data formatting | bytes 6553600 | tf_op jit(solution)/shard_map/while | solution.py:66
  32.9 5.4 %copy.33 = f32[2,2,8,160,160]{4,3,1,0,2:T(8,128)} copy(f32[2,2,8,160,160]{4,3,2,1,0:T(8,128)} %param.23) | data formatting | bytes 6553600 | tf_op jit(solution)/shard_map/while | solution.py:66
  39.5 10.4 %collective-permute-done.2 = f32[2,2,160,160]{3,2,1,0:T(8,128)} collective-permute-done((f32[2,2,160,160]{3,2,1,0:T(8,128)S(1)}, f32[2,2,160,160]{3,2,1,0:T(8,128)}, u32[]{:S(2)}, u32[]{:S(2)}) %collective-permute-start.2) | collective-permute-done | bytes 409632 | tf_op jit(solution)/shard_map/ppermute | solution.py:25
  51.0 3.1 %gather_fusion.1 = f32[16,2,160,160]{3,2,1,0:T(8,128)} fusion(f32[2,8,160,160]{3,2,1,0:T(8,128)S(1)} %constant_dynamic-update-slice_fusion.4, s32[1024]{0:T(1024)S(1)} %pad_clamp_fusion), kind=kCustom, calls=%fused_computation.1 | custom fusion | bytes 6553664 | tf_op jit(solution)/shard_map/gather | solution.py:101
  54.2 5.4 %copy.48 = f32[2,8,2,160,160]{4,3,0,2,1:T(8,128)} copy(f32[2,8,2,160,160]{4,3,2,1,0:T(8,128)} %bitcast.103) | data formatting | bytes 6553600 | tf_op jit(solution)/shard_map/gather | solution.py:101
  59.6 39.1 %while.41 = (s32[]{:T(128)}, f32[2,2,160,160]{3,2,1,0:T(8,128)S(1)}, s32[]{:T(128)}, f32[2,8]{0,1:T(8,128)S(1)}, f32[2,2,8,160,160]{4,3,1,0,2:T(8,128)}, /*index...) while((s32[]{:T(128)}, f32[2,2,160,160]{3,2,1,0:T(8,128)S(1)}, s32[]{:T(128)}, ...), condition=%wide.region_5.6_spmd, body=%wide.region_4.5_spmd.sunk | while | flops 393420800 | bytes 3605663 | solution.py:66
  62.4 2.1 fusion.91
  67.2 2.1 fusion.91
  72.0 2.1 fusion.91
  76.8 2.1 fusion.91
  81.6 2.1 fusion.91
  86.4 2.1 fusion.91
  91.2 2.1 fusion.91
  96.0 2.1 fusion.91
  98.7 5.0 %gather_fusion = f32[16,2,160,160]{3,2,1,0:T(8,128)} fusion(f32[8,2,160,160]{3,2,1,0:T(8,128)} %all-gather.3.cloned.1.call-done, s32[1024]{0:T(1024)S(1)} %pad_clamp_fusion.1), kind=kCustom, calls=%fused_computation | custom fusion | bytes 6553664 | tf_op jit(solution)/shard_map/gather | solution.py:100
  103.8 39.5 %while.40 = (s32[]{:T(128)}, f32[2,2,160,160]{3,2,1,0:T(8,128)S(1)}, s32[]{:T(128)}, f32[2,8]{0,1:T(8,128)S(1)}, f32[2,2,8,160,160]{4,3,1,0,2:T(8,128)}, /*index...) while((s32[]{:T(128)}, f32[2,2,160,160]{3,2,1,0:T(8,128)S(1)}, s32[]{:T(128)}, ...), condition=%wide.region_2.3_spmd, body=%wide.region_1.2_spmd.sunk | while | flops 393420800 | bytes 3605663 | solution.py:66
  106.7 2.1 fusion.84
  111.5 2.1 fusion.84
  116.4 2.1 fusion.84
  121.2 2.1 fusion.84
  126.1 2.1 fusion.84
  130.9 2.1 fusion.84
  135.8 2.1 fusion.84
  140.6 2.1 fusion.84
  147.0 24.2 %collective-permute-done.3 = f32[2,2,160,160]{3,2,1,0:T(8,128)S(1)} collective-permute-done((f32[2,2,160,160]{3,2,1,0:T(8,128)S(1)}, f32[2,2,160,160]{3,2,1,0:T(8,128)S(1)}, u32[]{:S(2)}, u32[]{:S(2)}) %collective-permute-start.3) | collective-permute-done | bytes 409632 | tf_op jit(solution)/shard_map/ppermute | solution.py:25
  173.0 12.7 %collective-permute-done.5 = f32[2,2,160,160]{3,2,1,0:T(8,128)S(1)} collective-permute-done((f32[2,2,160,160]{3,2,1,0:T(8,128)S(1)}, f32[2,2,160,160]{3,2,1,0:T(8,128)S(1)}, u32[]{:S(2)}, u32[]{:S(2)}) %collective-permute-start.5) | collective-permute-done | bytes 409632 | tf_op jit(solution)/shard_map/ppermute | solution.py:25
  186.6 4.9 %gather_fusion.3 = f32[16,2,160,160]{3,2,1,0:T(8,128)} fusion(f32[2,8,160,160]{3,2,1,0:T(8,128)} %constant_dynamic-update-slice_fusion, s32[1024]{0:T(1024)S(1)} %pad_clamp_fusion), kind=kCustom, calls=%fused_computation.3 | custom fusion | bytes 6553664 | tf_op jit(solution)/shard_map/gather | solution.py:101
  191.4 5.4 %copy.46 = f32[2,8,2,160,160]{4,3,0,2,1:T(8,128)} copy(f32[2,8,2,160,160]{4,3,2,1,0:T(8,128)} %bitcast.101) | data formatting | bytes 6553600 | tf_op jit(solution)/shard_map/gather | solution.py:101
  196.9 39.1 %while.43 = (s32[]{:T(128)}, f32[2,2,160,160]{3,2,1,0:T(8,128)S(1)}, s32[]{:T(128)}, f32[2,8]{0,1:T(8,128)S(1)}, f32[2,2,8,160,160]{4,3,1,0,2:T(8,128)}, /*index...) while((s32[]{:T(128)}, f32[2,2,160,160]{3,2,1,0:T(8,128)S(1)}, s32[]{:T(128)}, ...), condition=%wide.region_9.10_spmd, body=%wide.region_8.9_spmd.sunk | while | flops 393420800 | bytes 3605663 | solution.py:66
  199.7 2.1 fusion.105
  204.5 2.1 fusion.105
  209.3 2.1 fusion.105
  214.1 2.1 fusion.105
  218.9 2.1 fusion.105
  223.7 2.1 fusion.105
  228.5 2.1 fusion.105
  233.3 2.1 fusion.105
  236.0 5.0 %gather_fusion.2 = f32[16,2,160,160]{3,2,1,0:T(8,128)} fusion(f32[8,2,160,160]{3,2,1,0:T(8,128)} %all-gather.5.cloned.1.call-done, s32[1024]{0:T(1024)S(1)} %pad_clamp_fusion.1), kind=kCustom, calls=%fused_computation.2 | custom fusion | bytes 6553664 | tf_op jit(solution)/shard_map/gather | solution.py:100
  241.0 5.4 %copy.47 = f32[2,8,2,160,160]{4,3,2,0,1:T(8,128)} copy(f32[2,8,2,160,160]{4,3,2,1,0:T(8,128)} %bitcast.102) | data formatting | bytes 6553600 | tf_op jit(solution)/shard_map/gather | solution.py:100
  246.5 39.5 %while.42 = (s32[]{:T(128)}, f32[2,2,160,160]{3,2,1,0:T(8,128)S(1)}, s32[]{:T(128)}, f32[2,8]{0,1:T(8,128)S(1)}, f32[2,2,8,160,160]{4,3,1,0,2:T(8,128)}, /*index...) while((s32[]{:T(128)}, f32[2,2,160,160]{3,2,1,0:T(8,128)S(1)}, s32[]{:T(128)}, ...), condition=%wide.region_7.8_spmd, body=%wide.region_6.7_spmd.sunk | while | flops 393420800 | bytes 3605663 | solution.py:66
  249.3 2.1 fusion.98
  254.2 2.1 fusion.98
  259.0 2.1 fusion.98
  263.8 2.1 fusion.98
  268.7 2.1 fusion.98
  273.5 2.1 fusion.98
  278.4 2.1 fusion.98
  (121 shorter events, 89.0 us)
Async XLA Ops:
  7.2 91.6 %all-gather.3.cloned.1.call-start = ((), (), s32[]{:S(2)}) async-start(), calls=%async_computation | async-start | bytes 3276800 | tf_op jit(solution)/shard_map/all_gather | solution.py:98
  7.2 16.1 %collective-permute-start = (f32[2,2,160,160]{3,2,1,0:T(8,128)}, f32[2,2,160,160]{3,2,1,0:T(8,128)S(1)}, u32[]{:S(2)}, u32[]{:S(2)}) collective-permute-start(f32[2,2,160,160]{3,2,1,0:T(8,128)} %param.21), channel_id=1, source_target_pairs={{0,1},{1,2},{2,3},{3,0},{4,5},{5,6},{6,7},{7,4},{8,9},{9,10},{10,1... | collective-permute-start | bytes 1228808 | tf_op jit(solution)/shard_map/ppermute | solution.py:25
  8.6 29.8 %collective-permute-start.1 = (f32[2,2,160,160]{3,2,1,0:T(8,128)}, f32[2,2,160,160]{3,2,1,0:T(8,128)}, u32[]{:S(2)}, u32[]{:S(2)}) collective-permute-start(f32[2,2,160,160]{3,2,1,0:T(8,128)} %param.21), channel_id=1, source_target_pairs={{0,3},{1,0},{2,1},{3,2},{4,7},{5,4},{6,5},{7,6},{8,11},{9,8},{10,9... | collective-permute-start | bytes 1228808 | tf_op jit(solution)/shard_map/ppermute | solution.py:34
  8.8 227.3 %all-gather.5.cloned.1.call-start = ((), (), s32[]{:S(2)}) async-start(), calls=%async_computation.1 | async-start | bytes 3276800 | tf_op jit(solution)/shard_map/all_gather | solution.py:98
  23.3 26.6 %collective-permute-start.2 = (f32[2,2,160,160]{3,2,1,0:T(8,128)S(1)}, f32[2,2,160,160]{3,2,1,0:T(8,128)}, u32[]{:S(2)}, u32[]{:S(2)}) collective-permute-start(f32[2,2,160,160]{3,2,1,0:T(8,128)S(1)} %collective-permute-done), channel_id=1, source_target_pairs={{0,1},{1,2},{2,3},{3,0},{4,5},{5,6},{6,7},{7,4},{8,9},{9,10},{10,1... | collective-permute-start | bytes 1228808 | tf_op jit(solution)/shard_map/ppermute | solution.py:25
  103.8 39.9 %copy-start.1 = (f32[2,2,160,160]{3,2,1,0:T(8,128)S(1)}, f32[2,2,160,160]{3,2,1,0:T(8,128)}, u32[]{:S(2)}) copy-start(f32[2,2,160,160]{3,2,1,0:T(8,128)} %param.21) | copy-start | bytes 1228804
  103.8 39.9 %copy-start.4 = (f32[2,2,160,160]{3,2,1,0:T(8,128)S(1)}, f32[2,2,160,160]{3,2,1,0:T(8,128)}, u32[]{:S(2)}) copy-start(f32[2,2,160,160]{3,2,1,0:T(8,128)} %param.22) | copy-start | bytes 1228804
  103.8 39.9 %copy-start.5 = (f32[2,2,160]{2,1,0:T(2,128)S(1)}, f32[2,2,160]{2,1,0:T(2,128)}, u32[]{:S(2)}) copy-start(f32[2,2,160]{2,1,0:T(2,128)} %param.31) | copy-start | bytes 7684
  103.8 39.9 %copy-start.6 = (f32[2]{0:T(128)S(1)}, f32[2]{0:T(128)}, u32[]{:S(2)}) copy-start(f32[2]{0:T(128)} %param.33) | copy-start | bytes 28
  103.8 39.8 %copy-start.7 = (f32[2]{0:T(128)S(1)}, f32[2]{0:T(128)}, u32[]{:S(2)}) copy-start(f32[2]{0:T(128)} %param.32) | copy-start | bytes 28
  144.0 1.6 copy-start
  145.6 25.6 %copy-start.2 = (f32[2,2,160,160]{3,2,1,0:T(8,128)}, f32[2,2,160,160]{3,2,1,0:T(8,128)S(1)}, u32[]{:S(2)}) copy-start(f32[2,2,160,160]{3,2,1,0:T(8,128)S(1)} %get-tuple-element.261) | copy-start | bytes 1228804
  145.6 25.6 %collective-permute-start.3 = (f32[2,2,160,160]{3,2,1,0:T(8,128)S(1)}, f32[2,2,160,160]{3,2,1,0:T(8,128)S(1)}, u32[]{:S(2)}, u32[]{:S(2)}) collective-permute-start(f32[2,2,160,160]{3,2,1,0:T(8,128)S(1)} %get-tuple-element.261), channel_id=1, source_target_pairs={{0,1},{1,2},{2,3},{3,0},{4,5},{5,6},{6,7},{7,4},{8,9},{9,10},{10,1... | collective-permute-start | bytes 1228808 | tf_op jit(solution)/shard_map/ppermute | solution.py:25
  145.6 26.5 %collective-permute-start.4 = (f32[2,2,160,160]{3,2,1,0:T(8,128)S(1)}, f32[2,2,160,160]{3,2,1,0:T(8,128)S(1)}, u32[]{:S(2)}, u32[]{:S(2)}) collective-permute-start(f32[2,2,160,160]{3,2,1,0:T(8,128)S(1)} %get-tuple-element.261), channel_id=1, source_target_pairs={{0,3},{1,0},{2,1},{3,2},{4,7},{5,4},{6,5},{7,6},{8,11},{9,8},{10,9... | collective-permute-start | bytes 1228808 | tf_op jit(solution)/shard_map/ppermute | solution.py:34
  171.2 14.5 %collective-permute-start.5 = (f32[2,2,160,160]{3,2,1,0:T(8,128)S(1)}, f32[2,2,160,160]{3,2,1,0:T(8,128)S(1)}, u32[]{:S(2)}, u32[]{:S(2)}) collective-permute-start(f32[2,2,160,160]{3,2,1,0:T(8,128)S(1)} %collective-permute-done.3), channel_id=1, source_target_pairs={{0,1},{1,2},{2,3},{3,0},{4,5},{5,6},{6,7},{7,4},{8,9},{9,10},{10,1... | collective-permute-start | bytes 1228808 | tf_op jit(solution)/shard_map/ppermute | solution.py:25
  246.5 39.5 %copy-start.3 = (f32[2,2,160,160]{3,2,1,0:T(8,128)S(1)}, f32[2,2,160,160]{3,2,1,0:T(8,128)}, u32[]{:S(2)}) copy-start(f32[2,2,160,160]{3,2,1,0:T(8,128)} %copy-done.2) | copy-start | bytes 1228804
Sparse Core Ops, SparseCore 0:
  9.5 26.0 all-gather.2
  171.4 23.8 all-gather.4
